TPU v7x, 256 devices: a whole 4x4x8 slice. The times are simulated.
256 devices in a mesh: req: 64 (over z, x, core), ffn: 4 (over y).
Axes of the slice: x: 4, y: 4, z: 8, core: 2. Of those that a mesh axis runs over, the one named last changes fastest.
Arguments:
- residual: bfloat16 [16384, 2048], P('req')
- queries: bfloat16 [16384, 4096], P('req', 'ffn')
- rotated_key_rows: bfloat16 [16384, 2048], P('req', 'ffn')
- values: bfloat16 [16384, 2048], P('req', 'ffn'), may hold values from -6 to 6
- req_start: int32 [16384], P('req'), may hold values from 0 to 16383, as said below
- head_sink_logit: float32 [32], P('ffn'), may hold values from 6 to 11
- out_proj: bfloat16 [4096, 2048], P('ffn', 'req'), may hold values from -0.25 to 0.25
- mid_gain: float32 [2048], replicated, may hold values from 0.1 to 1.9
- router_logits: float32 [16384, 8], P('req')
- routes: int32 [16384, 2], P('req'), may hold values from 0 to 63, as said below
- placement: int32 [64], replicated, may hold values from 0 to 7, as said below
- w_gate: bfloat16 [64, 2048, 3072], P('req', None, 'ffn'), as said below
- w_up: bfloat16 [64, 2048, 3072], P('req', None, 'ffn'), as said below
- w_down: bfloat16 [64, 2048, 3072], P('req', None, 'ffn'), as said below
Outputs:
- layer_out: bfloat16 [16384, 2048], P('req', 'ffn')
Inputs may be any that keep to these rules, and one draw needn't show every extreme that they name: req_start[p] is the first position of the request that holds position p; requests are runs of consecutive positions, each at most 8192 long, one is exactly 8192 long, and the last position is a request of one token. `routes`: the two entries of a token name indices that host different experts. Among the 512 entries of the tokens of one index of req, an index appears at most 10 times, and every index that hosts one certain expert appears exactly 10 times, in every such block. `placement`: every expert is hosted at one index or more. `w_gate`: rows k and m are equal where placement[k] == placement[m]. `w_up`: rows k and m are equal where placement[k] == placement[m]. `w_down`: rows k and m are equal where placement[k] == placement[m].
All inputs are finite; a program needn't handle non-finite values.
Results may differ from a plain program's by a relative error of at most 0.0075.
Values may be sent and summed in bfloat16 or wider, within the bound.
A program may use at most 128 MiB of HBM per device.

v0:
```python
import jax
import jax.numpy as jnp
from jax import lax
from jax.sharding import PartitionSpec as P

QUERY_HEADS = 32
KEY_VALUE_HEADS = 16
HEAD_SIZE = 128
EXPERTS = 8


EPS = 1e-06


def shifted(value, axis, steps):
    count = lax.axis_size(axis)
    initial, last = (max(0, -steps), min(count, count - steps))
    return lax.ppermute(value, axis, [(source, source + steps) for source in range(initial, last)])


def step_back(keys_in_block, values_in_block):
    return shifted((keys_in_block, values_in_block), "req", 1)


def per_device(
    residual,
    queries,
    rotated_key_rows,
    values,
    req_start,
    head_sink_logit,
    out_proj,
    mid_gain,
    router_logits,
    routes,
    placement,
    w_gate,
    w_up,
    w_down,
):
    tok_count = residual.shape[0]
    model_width = residual.shape[1]
    req_size = lax.axis_size("req")
    ffn_size = lax.axis_size("ffn")
    own_req = lax.axis_index("req")
    own_ffn = lax.axis_index("ffn")
    query_group_width = QUERY_HEADS // KEY_VALUE_HEADS
    kv_heads = rotated_key_rows.shape[1] // HEAD_SIZE
    quarter = model_width // ffn_size
    gate_mat = w_gate[0]
    up_mat = w_up[0]
    down_mat = w_down[0]
    shard_queries = queries.reshape(tok_count, kv_heads, query_group_width, HEAD_SIZE)
    local_keys = rotated_key_rows.reshape(tok_count, kv_heads, HEAD_SIZE)
    local_values = values.reshape(tok_count, kv_heads, HEAD_SIZE)
    win_span = min(16, req_size // 2)
    window = win_span * tok_count
    query_pos = own_req * tok_count + jnp.arange(tok_count, dtype=jnp.int32)
    logit_scale_factor = HEAD_SIZE ** (-0.5)

    def attend(carry_state, keys_in_block, values_in_block, key_first):
        running_max, row_total, weighted_value_sum = carry_state
        attention_logits = (
            jnp.einsum(
                "veck,uek->ecvu", shard_queries, keys_in_block, preferred_element_type=jnp.float32
            )
            * logit_scale_factor
        )
        key_pos = key_first + jnp.arange(keys_in_block.shape[0], dtype=jnp.int32)
        visible = (
            (key_pos[None, :] >= req_start[:, None])
            & (key_pos[None, :] <= query_pos[:, None])
            & (query_pos[:, None] - key_pos[None, :] < window)
        )
        attention_logits = jnp.where(visible[None, None], attention_logits, -jnp.inf)
        new_max = jnp.maximum(running_max, jnp.max(attention_logits, axis=-1))
        probs = jnp.exp(attention_logits - new_max[..., None])
        factor = jnp.exp(running_max - new_max)
        row_total = row_total * factor + jnp.sum(probs, axis=-1)
        weighted_value_sum = weighted_value_sum * factor[..., None] + jnp.einsum(
            "plyw,wpj->plyj",
            probs.astype(jnp.bfloat16),
            values_in_block,
            preferred_element_type=jnp.float32,
        )
        return (new_max, row_total, weighted_value_sum)

    initial_sink_logit = jnp.broadcast_to(
        head_sink_logit.reshape(kv_heads, query_group_width, 1),
        (kv_heads, query_group_width, tok_count),
    )
    carry_state = (
        initial_sink_logit,
        jnp.ones((kv_heads, query_group_width, tok_count), jnp.float32),
        jnp.zeros((kv_heads, query_group_width, tok_count, HEAD_SIZE), jnp.float32),
    )
    carry_state = attend(carry_state, local_keys, local_values, own_req * tok_count)
    pair_count = win_span // 2

    def pair_step(step_idx, loop_carry):
        folded, near_keys, near_values = loop_carry
        mid_keys, mid_values = step_back(near_keys, near_values)
        far_keys, far_values = step_back(mid_keys, mid_values)
        key_first = (own_req - 2 * step_idx - 2) * tok_count
        folded = attend(
            folded,
            jnp.concatenate([far_keys, mid_keys], 0),
            jnp.concatenate([far_values, mid_values], 0),
            key_first,
        )
        return (folded, far_keys, far_values)

    carry_state, unused_keys, unused_values = lax.fori_loop(
        0, pair_count, pair_step, (carry_state, local_keys, local_values)
    )
    running_max, row_total, weighted_value_sum = carry_state
    attended = (weighted_value_sum / row_total[..., None]).astype(jnp.bfloat16)
    flat_attended = jnp.transpose(attended, (2, 0, 1, 3)).reshape(tok_count, -1)
    proj = jnp.dot(
        flat_attended,
        lax.all_gather(out_proj, "req", axis=1, tiled=True),
        preferred_element_type=jnp.float32,
    )
    summed = lax.psum(proj.astype(jnp.bfloat16), "ffn").astype(jnp.float32)
    hidden_state = residual.astype(jnp.float32) + summed
    mean_sq = jnp.mean(hidden_state * hidden_state, axis=1, keepdims=True)
    normed = (hidden_state * lax.rsqrt(mean_sq + EPS) * mid_gain).astype(jnp.bfloat16)
    own_hidden = lax.dynamic_slice_in_dim(hidden_state, own_ffn * quarter, quarter, 1)
    capacity = 5 * tok_count // (2 * req_size)
    flat_routes = routes.reshape(-1)
    slot_iota = jnp.arange(req_size, dtype=jnp.int32)
    dest_hot = (flat_routes[:, None] == slot_iota[None, :]).astype(jnp.int32)
    slot_depth = jnp.sum((jnp.cumsum(dest_hot, axis=0) - dest_hot) * dest_hot, axis=1)
    slot_index = flat_routes * capacity + slot_depth
    row_tokens = jnp.arange(2 * tok_count, dtype=jnp.int32) // 2
    send_rows = (
        jnp.zeros((req_size * capacity, model_width), jnp.bfloat16)
        .at[slot_index]
        .set(normed[row_tokens])
    )
    send_rows = send_rows.reshape(req_size, capacity, model_width)
    arrived = lax.all_to_all(send_rows, "req", split_axis=0, concat_axis=0, tiled=True)
    flat_rows = arrived.reshape(-1, model_width)
    gate_val = jnp.dot(flat_rows, gate_mat, preferred_element_type=jnp.float32)
    up_val = jnp.dot(flat_rows, up_mat, preferred_element_type=jnp.float32)
    activated = (jax.nn.silu(gate_val) * up_val).astype(jnp.bfloat16)
    partial_out = lax.dot_general(
        activated, down_mat, (((1,), (1,)), ((), ())), preferred_element_type=jnp.float32
    )
    partial_rows = partial_out.astype(jnp.bfloat16).reshape(
        arrived.shape[0], arrived.shape[1], model_width
    )
    returned_parts = lax.all_to_all(
        lax.all_to_all(partial_rows[None], "req", split_axis=1, concat_axis=1, tiled=True),
        "ffn",
        split_axis=3,
        concat_axis=0,
        tiled=True,
    )
    returned = jnp.sum(returned_parts.astype(jnp.float32), axis=0)
    expert_of = jnp.sum(dest_hot * placement[None, :], axis=1).reshape(tok_count, 2)
    expert_hot = (
        expert_of[:, :, None] == jnp.arange(EXPERTS, dtype=jnp.int32)[None, None, :]
    ).astype(jnp.float32)
    chosen = jnp.sum(router_logits[:, None, :] * expert_hot, axis=2)
    logit_peak = jnp.max(chosen, axis=1, keepdims=True)
    exp_logits = jnp.exp(chosen - logit_peak)
    gate_weights = exp_logits / jnp.sum(exp_logits, axis=1, keepdims=True)
    picked = returned.reshape(req_size * capacity, quarter)[slot_index].reshape(
        tok_count, 2, quarter
    )
    mixture = jnp.sum(picked * gate_weights[:, :, None], axis=1)
    return (own_hidden + mixture).astype(jnp.bfloat16)


def solution(mesh):
    in_specs = (
        P("req", None),
        P("req", "ffn"),
        P("req", "ffn"),
        P("req", "ffn"),
        P("req"),
        P("ffn"),
        P("ffn", "req"),
        P(),
        P("req", None),
        P("req", None),
        P(),
        P("req", None, "ffn"),
        P("req", None, "ffn"),
        P("req", None, "ffn"),
    )
    out_specs = P("req", "ffn")
    return jax.shard_map(
        per_device, mesh=mesh, in_specs=in_specs, out_specs=out_specs, check_vma=False
    )
```

profile of v0, /device:TPU:32, one launch (start us, length us, event | category | flops | bytes accessed | tf_op | source)
XLA Modules:
  0.0 686.9 jit_solution(4302674995303318617)
XLA Ops:
  8.6 2.0 copy.102
  12.5 2.0 copy.110
  22.4 3.3 convolution_add_fusion
  25.7 217.4 %while.24 = (s32[]{:T(128)}, f32[4,2,256]{2,1,0:T(2,128)S(1)}, f32[4,2,256]{2,1,0:T(2,128)S(1)}, f32[4,2,256,128]{3,2,1,0:T(8,128)}, bf16[256,4,128]{2,0,1:T(8,1...) while((s32[]{:T(128)}, f32[4,2,256]{2,1,0:T(2,128)S(1)}, ...), condition=%wide.region_5.6_spmd.clone, body=%wide.region_2.5_spmd.clone.sunk | while | flops 551817984 | bytes 30547376 | solution.py:113
  27.6 3.5 collective-permute-start.2
  31.1 4.8 collective-permute-done
  41.2 5.1 collective-permute-done.1
  49.6 2.6 fusion.70
  55.2 1.9 collective-permute-start.2
  57.1 6.0 collective-permute-done
  65.3 2.2 collective-permute-done.2
  69.4 5.7 collective-permute-done.1
  75.1 1.9 fusion.68
  77.9 2.3 collective-permute-done.3
  80.2 2.6 fusion.70
  85.7 1.9 collective-permute-start.2
  87.7 6.0 collective-permute-done
  98.5 5.3 collective-permute-done.1
  106.8 2.5 fusion.70
  112.3 1.9 collective-permute-start.2
  114.2 6.0 collective-permute-done
  125.0 5.3 collective-permute-done.1
  133.4 2.5 fusion.70
  138.8 1.9 collective-permute-start.2
  140.8 6.0 collective-permute-done
  151.5 5.3 collective-permute-done.1
  159.9 2.5 fusion.70
  165.4 1.9 collective-permute-start.2
  167.3 6.0 collective-permute-done
  178.1 5.3 collective-permute-done.1
  186.5 2.5 fusion.70
  191.9 1.9 collective-permute-start.2
  193.9 6.0 collective-permute-done
  204.6 5.3 collective-permute-done.1
  213.0 2.5 fusion.70
  218.5 1.9 collective-permute-start.2
  220.4 6.0 collective-permute-done
  231.2 5.3 collective-permute-done.1
  239.6 2.5 fusion.70
  243.1 2.5 copy.111
  245.7 2.1 divide_convert_fusion
  247.8 4.7 convolution_convert_fusion.1
  254.9 69.6 %all-reduce.2.cloned.1.call-done = bf16[256,2048]{1,0:T(8,128)(2,1)} async-done(((bf16[256,2048]{1,0:T(8,128)(2,1)}), bf16[256,2048]{1,0:T(8,128)(2,1)}) %all-reduce.2.cloned.1.call-update) | async-done | bytes 1048592 | tf_op jit(solution)/shard_map/psum | solution.py:124
  324.5 3.4 convert_add_fusion
  329.4 11.3 %scatter_custom_fusion = bf16[640,2048]{1,0:T(8,128)(2,1)} fusion(s32[512]{0:T(512)S(1)} %bitcast.136, bf16[256,2048]{1,0:T(8,128)(2,1)} %multiply_convert_fusion, s32[1024]{0:T(1024)S(1)} %pad_clamp_fusion.1, bf16[]{:T(256)} %constant.128.clone.1), kind=kCustom, calls=%fused_computation.40 | custom fusion | bytes 2621952 | tf_op jit(solution)/shard_map/scatter | solution.py:139
  340.7 5.4 reshape.364
  346.1 106.1 %all_to_all.19 = bf16[64,10,2048]{2,1,0:T(8,128)(2,1)} all-to-all(bf16[64,10,2048]{2,1,0:T(8,128)(2,1)} %reshape.364), channel_id=1, replica_groups=mesh['req'=64,'ffn'=4] {'req'}, dimensions={0} | all-to-all | bytes 5242880 | tf_op jit(solution)/shard_map/all_to_all | solution.py:142
  452.2 5.5 reshape.365
  457.7 6.2 fusion.27
  463.9 9.7 %convolution_convert_fusion = bf16[640,2048]{1,0:T(8,128)(2,1)} fusion(bf16[1,2048,768]{2,1,0:T(8,128)(2,1)S(1)} %copy-done, f32[640,768]{1,0:T(8,128)} %fusion.27, bf16[640,2048]{1,0:T(8,128)(2,1)} %reshape.365, bf16[1,2048,768]{2,1,0:T(8,128)(2,1)} %param.28), kind=kOutput, calls=%fused_computation.32 | convolution fusion | flops 4030791680 | bytes 13500416 | tf_op jit(solution)/shard_map/dot_general | solution.py:147
  473.6 5.4 broadcast_in_dim_reshape.2
  478.9 101.8 %all_to_all.20 = bf16[1,64,10,2048]{3,2,0,1:T(8,128)(2,1)} all-to-all(bf16[1,64,10,2048]{3,2,0,1:T(8,128)(2,1)} %bitcast.121), channel_id=1, replica_groups=mesh['req'=64,'ffn'=4] {'req'}, dimensions={1} | all-to-all | bytes 5242880 | tf_op jit(solution)/shard_map/all_to_all | solution.py:154
  580.8 14.3 %copy.117 = bf16[1,64,10,2048]{1,2,0,3:T(8,128)(2,1)} copy(bf16[1,64,10,2048]{3,2,0,1:T(8,128)(2,1)} %all_to_all.20) | data formatting | bytes 5242880 | tf_op jit(solution)/shard_map/all_to_all | solution.py:154
  595.1 7.5 %reshape.404 = bf16[4,2,163840]{2,1,0:T(2,128)(2,1)} reshape(bf16[2048,1,10,64]{3,2,1,0:T(8,128)(2,1)} %bitcast.119) | data formatting | bytes 5242880
  602.6 4.3 all-to-all-start.2
  607.4 31.6 %all-to-all-done.2 = bf16[4,2,163840]{2,1,0:T(2,128)(2,1)S(1)} async-done(((bf16[4,2,163840]{2,1,0:T(2,128)(2,1)}), bf16[4,2,163840]{2,1,0:T(2,128)(2,1)S(1)}, u32[]{:S(2)}, u32[]{:S(2)}) %all-to-all-start.2) | async-done | bytes 2621472 | tf_op jit(solution)/shard_map/all_to_all | solution.py:153
  638.9 5.8 reshape.405
  644.8 7.9 %copy.118 = bf16[1,64,10,2048]{3,1,2,0:T(8,128)(2,1)S(1)} copy(bf16[1,64,10,2048]{1,2,0,3:T(8,128)(2,1)} %bitcast.120) | data formatting | bytes 5242880 | tf_op jit(solution)/shard_map/all_to_all | solution.py:153
  652.6 5.5 reshape.368
  658.1 6.8 reduce_sum.94
  665.0 2.1 copy.119
  668.3 4.2 gather_fusion
  672.5 2.8 reshape.367
  675.4 2.6 multiply_reduce_fusion.1
  (214 shorter events, 102.3 us)
Async XLA Ops:
  6.5 457.4 %copy-start = (bf16[1,2048,768]{2,1,0:T(8,128)(2,1)S(1)}, bf16[1,2048,768]{2,1,0:T(8,128)(2,1)}, u32[]{:S(2)}) copy-start(bf16[1,2048,768]{2,1,0:T(8,128)(2,1)} %param.29) | copy-start | bytes 9437188
  6.5 8.0 %copy-start.9 = (s32[256]{0:T(256)S(1)}, s32[256]{0:T(256)}, u32[]{:S(2)}) copy-start(s32[256]{0:T(256)} %param.20) | copy-start | bytes 3076
  6.5 241.2 %all-gather.2.cloned.1.call-start = ((), (), s32[]{:S(2)}) async-start(), calls=%async_computation.3 | async-start | bytes 4259840 | tf_op jit(solution)/shard_map/all_gather | solution.py:121
  7.3 317.2 %all-reduce.2.cloned.1.call-start = ((), (), s32[]{:S(2)}) async-start(), calls=%async_computation.4 | async-start | bytes 2097152 | tf_op jit(solution)/shard_map/psum | solution.py:124
  16.2 1.3 copy-start.2
  20.6 5.1 copy-start.7
  25.7 10.2 %collective-permute-start = (bf16[256,4,128]{2,0,1:T(8,128)(2,1)S(1)}, bf16[256,4,128]{2,0,1:T(8,128)(2,1)}, u32[]{:S(2)}, u32[]{:S(2)}) collective-permute-start(bf16[256,4,128]{2,0,1:T(8,128)(2,1)S(1)} %get-tuple-element.446), channel_id=1, source_target_pairs={{0,4},{4,8},{8,12},{12,16},{16,20},{20,24},{24,28},{28,32},{32,36}... | collective-permute-start | bytes 786440 | tf_op jit(solution)/shard_map/while/body/eval_jaxpr/ppermute | solution.py:18
  27.6 11.7 %collective-permute-start.2 = (bf16[256,4,128]{2,0,1:T(8,128)(2,1)}, bf16[256,4,128]{2,0,1:T(8,128)(2,1)}, u32[]{:S(2)}, u32[]{:S(2)}) collective-permute-start(bf16[256,4,128]{2,0,1:T(8,128)(2,1)} %get-tuple-element.447), channel_id=1, source_target_pairs={{0,4},{4,8},{8,12},{12,16},{16,20},{20,24},{24,28},{28,32},{32,36}... | collective-permute-start | bytes 786440 | tf_op jit(solution)/shard_map/while/body/eval_jaxpr/ppermute | solution.py:18
  35.9 10.4 %collective-permute-start.1 = (bf16[256,4,128]{2,0,1:T(8,128)(2,1)}, bf16[256,4,128]{2,0,1:T(8,128)(2,1)S(1)}, u32[]{:S(2)}, u32[]{:S(2)}) collective-permute-start(bf16[256,4,128]{2,0,1:T(8,128)(2,1)} %collective-permute-done), channel_id=1, source_target_pairs={{0,4},{4,8},{8,12},{12,16},{16,20},{20,24},{24,28},{28,32},{32,36}... | collective-permute-start | bytes 786440 | tf_op jit(solution)/shard_map/while/body/eval_jaxpr/ppermute | solution.py:18
  39.3 10.3 %collective-permute-start.3 = (bf16[256,4,128]{2,0,1:T(8,128)(2,1)}, bf16[256,4,128]{2,0,1:T(8,128)(2,1)S(1)}, u32[]{:S(2)}, u32[]{:S(2)}) collective-permute-start(bf16[256,4,128]{2,0,1:T(8,128)(2,1)} %collective-permute-done.2), channel_id=1, source_target_pairs={{0,4},{4,8},{8,12},{12,16},{16,20},{20,24},{24,28},{28,32},{32,36}... | collective-permute-start | bytes 786440 | tf_op jit(solution)/shard_map/while/body/eval_jaxpr/ppermute | solution.py:18
  48.2 1.4 copy-start.5
  49.6 2.6 copy-start.8
  53.3 9.9 %collective-permute-start = (bf16[256,4,128]{2,0,1:T(8,128)(2,1)S(1)}, bf16[256,4,128]{2,0,1:T(8,128)(2,1)}, u32[]{:S(2)}, u32[]{:S(2)}) collective-permute-start(bf16[256,4,128]{2,0,1:T(8,128)(2,1)S(1)} %get-tuple-element.446), channel_id=1, source_target_pairs={{0,4},{4,8},{8,12},{12,16},{16,20},{20,24},{24,28},{28,32},{32,36}... | collective-permute-start | bytes 786440 | tf_op jit(solution)/shard_map/while/body/eval_jaxpr/ppermute | solution.py:18
  55.2 12.3 %collective-permute-start.2 = (bf16[256,4,128]{2,0,1:T(8,128)(2,1)}, bf16[256,4,128]{2,0,1:T(8,128)(2,1)}, u32[]{:S(2)}, u32[]{:S(2)}) collective-permute-start(bf16[256,4,128]{2,0,1:T(8,128)(2,1)} %get-tuple-element.447), channel_id=1, source_target_pairs={{0,4},{4,8},{8,12},{12,16},{16,20},{20,24},{24,28},{28,32},{32,36}... | collective-permute-start | bytes 786440 | tf_op jit(solution)/shard_map/while/body/eval_jaxpr/ppermute | solution.py:18
  63.2 11.9 %collective-permute-start.1 = (bf16[256,4,128]{2,0,1:T(8,128)(2,1)}, bf16[256,4,128]{2,0,1:T(8,128)(2,1)S(1)}, u32[]{:S(2)}, u32[]{:S(2)}) collective-permute-start(bf16[256,4,128]{2,0,1:T(8,128)(2,1)} %collective-permute-done), channel_id=1, source_target_pairs={{0,4},{4,8},{8,12},{12,16},{16,20},{20,24},{24,28},{28,32},{32,36}... | collective-permute-start | bytes 786440 | tf_op jit(solution)/shard_map/while/body/eval_jaxpr/ppermute | solution.py:18
  67.5 12.7 %collective-permute-start.3 = (bf16[256,4,128]{2,0,1:T(8,128)(2,1)}, bf16[256,4,128]{2,0,1:T(8,128)(2,1)S(1)}, u32[]{:S(2)}, u32[]{:S(2)}) collective-permute-start(bf16[256,4,128]{2,0,1:T(8,128)(2,1)} %collective-permute-done.2), channel_id=1, source_target_pairs={{0,4},{4,8},{8,12},{12,16},{16,20},{20,24},{24,28},{28,32},{32,36}... | collective-permute-start | bytes 786440 | tf_op jit(solution)/shard_map/while/body/eval_jaxpr/ppermute | solution.py:18
  77.0 3.2 copy-start.5
  80.2 2.6 copy-start.8
  82.8 1.0 copy-start.6
  83.8 9.9 %collective-permute-start = (bf16[256,4,128]{2,0,1:T(8,128)(2,1)S(1)}, bf16[256,4,128]{2,0,1:T(8,128)(2,1)}, u32[]{:S(2)}, u32[]{:S(2)}) collective-permute-start(bf16[256,4,128]{2,0,1:T(8,128)(2,1)S(1)} %get-tuple-element.446), channel_id=1, source_target_pairs={{0,4},{4,8},{8,12},{12,16},{16,20},{20,24},{24,28},{28,32},{32,36}... | collective-permute-start | bytes 786440 | tf_op jit(solution)/shard_map/while/body/eval_jaxpr/ppermute | solution.py:18
  85.7 10.8 %collective-permute-start.2 = (bf16[256,4,128]{2,0,1:T(8,128)(2,1)}, bf16[256,4,128]{2,0,1:T(8,128)(2,1)}, u32[]{:S(2)}, u32[]{:S(2)}) collective-permute-start(bf16[256,4,128]{2,0,1:T(8,128)(2,1)} %get-tuple-element.447), channel_id=1, source_target_pairs={{0,4},{4,8},{8,12},{12,16},{16,20},{20,24},{24,28},{28,32},{32,36}... | collective-permute-start | bytes 786440 | tf_op jit(solution)/shard_map/while/body/eval_jaxpr/ppermute | solution.py:18
  93.7 10.0 %collective-permute-start.1 = (bf16[256,4,128]{2,0,1:T(8,128)(2,1)}, bf16[256,4,128]{2,0,1:T(8,128)(2,1)S(1)}, u32[]{:S(2)}, u32[]{:S(2)}) collective-permute-start(bf16[256,4,128]{2,0,1:T(8,128)(2,1)} %collective-permute-done), channel_id=1, source_target_pairs={{0,4},{4,8},{8,12},{12,16},{16,20},{20,24},{24,28},{28,32},{32,36}... | collective-permute-start | bytes 786440 | tf_op jit(solution)/shard_map/while/body/eval_jaxpr/ppermute | solution.py:18
  96.5 10.0 %collective-permute-start.3 = (bf16[256,4,128]{2,0,1:T(8,128)(2,1)}, bf16[256,4,128]{2,0,1:T(8,128)(2,1)S(1)}, u32[]{:S(2)}, u32[]{:S(2)}) collective-permute-start(bf16[256,4,128]{2,0,1:T(8,128)(2,1)} %collective-permute-done.2), channel_id=1, source_target_pairs={{0,4},{4,8},{8,12},{12,16},{16,20},{20,24},{24,28},{28,32},{32,36}... | collective-permute-start | bytes 786440 | tf_op jit(solution)/shard_map/while/body/eval_jaxpr/ppermute | solution.py:18
  105.6 1.2 copy-start.5
  106.5 2.8 copy-start.8
  109.4 1.0 copy-start.6
  110.4 9.9 %collective-permute-start = (bf16[256,4,128]{2,0,1:T(8,128)(2,1)S(1)}, bf16[256,4,128]{2,0,1:T(8,128)(2,1)}, u32[]{:S(2)}, u32[]{:S(2)}) collective-permute-start(bf16[256,4,128]{2,0,1:T(8,128)(2,1)S(1)} %get-tuple-element.446), channel_id=1, source_target_pairs={{0,4},{4,8},{8,12},{12,16},{16,20},{20,24},{24,28},{28,32},{32,36}... | collective-permute-start | bytes 786440 | tf_op jit(solution)/shard_map/while/body/eval_jaxpr/ppermute | solution.py:18
  112.3 10.8 %collective-permute-start.2 = (bf16[256,4,128]{2,0,1:T(8,128)(2,1)}, bf16[256,4,128]{2,0,1:T(8,128)(2,1)}, u32[]{:S(2)}, u32[]{:S(2)}) collective-permute-start(bf16[256,4,128]{2,0,1:T(8,128)(2,1)} %get-tuple-element.447), channel_id=1, source_target_pairs={{0,4},{4,8},{8,12},{12,16},{16,20},{20,24},{24,28},{28,32},{32,36}... | collective-permute-start | bytes 786440 | tf_op jit(solution)/shard_map/while/body/eval_jaxpr/ppermute | solution.py:18
  120.3 10.0 %collective-permute-start.1 = (bf16[256,4,128]{2,0,1:T(8,128)(2,1)}, bf16[256,4,128]{2,0,1:T(8,128)(2,1)S(1)}, u32[]{:S(2)}, u32[]{:S(2)}) collective-permute-start(bf16[256,4,128]{2,0,1:T(8,128)(2,1)} %collective-permute-done), channel_id=1, source_target_pairs={{0,4},{4,8},{8,12},{12,16},{16,20},{20,24},{24,28},{28,32},{32,36}... | collective-permute-start | bytes 786440 | tf_op jit(solution)/shard_map/while/body/eval_jaxpr/ppermute | solution.py:18
  123.1 10.0 %collective-permute-start.3 = (bf16[256,4,128]{2,0,1:T(8,128)(2,1)}, bf16[256,4,128]{2,0,1:T(8,128)(2,1)S(1)}, u32[]{:S(2)}, u32[]{:S(2)}) collective-permute-start(bf16[256,4,128]{2,0,1:T(8,128)(2,1)} %collective-permute-done.2), channel_id=1, source_target_pairs={{0,4},{4,8},{8,12},{12,16},{16,20},{20,24},{24,28},{28,32},{32,36}... | collective-permute-start | bytes 786440 | tf_op jit(solution)/shard_map/while/body/eval_jaxpr/ppermute | solution.py:18
  132.2 1.2 copy-start.5
  133.1 2.8 copy-start.8
  136.9 9.9 %collective-permute-start = (bf16[256,4,128]{2,0,1:T(8,128)(2,1)S(1)}, bf16[256,4,128]{2,0,1:T(8,128)(2,1)}, u32[]{:S(2)}, u32[]{:S(2)}) collective-permute-start(bf16[256,4,128]{2,0,1:T(8,128)(2,1)S(1)} %get-tuple-element.446), channel_id=1, source_target_pairs={{0,4},{4,8},{8,12},{12,16},{16,20},{20,24},{24,28},{28,32},{32,36}... | collective-permute-start | bytes 786440 | tf_op jit(solution)/shard_map/while/body/eval_jaxpr/ppermute | solution.py:18
  138.8 10.8 %collective-permute-start.2 = (bf16[256,4,128]{2,0,1:T(8,128)(2,1)}, bf16[256,4,128]{2,0,1:T(8,128)(2,1)}, u32[]{:S(2)}, u32[]{:S(2)}) collective-permute-start(bf16[256,4,128]{2,0,1:T(8,128)(2,1)} %get-tuple-element.447), channel_id=1, source_target_pairs={{0,4},{4,8},{8,12},{12,16},{16,20},{20,24},{24,28},{28,32},{32,36}... | collective-permute-start | bytes 786440 | tf_op jit(solution)/shard_map/while/body/eval_jaxpr/ppermute | solution.py:18
  146.8 10.0 %collective-permute-start.1 = (bf16[256,4,128]{2,0,1:T(8,128)(2,1)}, bf16[256,4,128]{2,0,1:T(8,128)(2,1)S(1)}, u32[]{:S(2)}, u32[]{:S(2)}) collective-permute-start(bf16[256,4,128]{2,0,1:T(8,128)(2,1)} %collective-permute-done), channel_id=1, source_target_pairs={{0,4},{4,8},{8,12},{12,16},{16,20},{20,24},{24,28},{28,32},{32,36}... | collective-permute-start | bytes 786440 | tf_op jit(solution)/shard_map/while/body/eval_jaxpr/ppermute | solution.py:18
  149.6 10.0 %collective-permute-start.3 = (bf16[256,4,128]{2,0,1:T(8,128)(2,1)}, bf16[256,4,128]{2,0,1:T(8,128)(2,1)S(1)}, u32[]{:S(2)}, u32[]{:S(2)}) collective-permute-start(bf16[256,4,128]{2,0,1:T(8,128)(2,1)} %collective-permute-done.2), channel_id=1, source_target_pairs={{0,4},{4,8},{8,12},{12,16},{16,20},{20,24},{24,28},{28,32},{32,36}... | collective-permute-start | bytes 786440 | tf_op jit(solution)/shard_map/while/body/eval_jaxpr/ppermute | solution.py:18
  158.7 1.2 copy-start.5
  159.6 2.8 copy-start.8
  163.5 9.9 %collective-permute-start = (bf16[256,4,128]{2,0,1:T(8,128)(2,1)S(1)}, bf16[256,4,128]{2,0,1:T(8,128)(2,1)}, u32[]{:S(2)}, u32[]{:S(2)}) collective-permute-start(bf16[256,4,128]{2,0,1:T(8,128)(2,1)S(1)} %get-tuple-element.446), channel_id=1, source_target_pairs={{0,4},{4,8},{8,12},{12,16},{16,20},{20,24},{24,28},{28,32},{32,36}... | collective-permute-start | bytes 786440 | tf_op jit(solution)/shard_map/while/body/eval_jaxpr/ppermute | solution.py:18
  165.4 10.8 %collective-permute-start.2 = (bf16[256,4,128]{2,0,1:T(8,128)(2,1)}, bf16[256,4,128]{2,0,1:T(8,128)(2,1)}, u32[]{:S(2)}, u32[]{:S(2)}) collective-permute-start(bf16[256,4,128]{2,0,1:T(8,128)(2,1)} %get-tuple-element.447), channel_id=1, source_target_pairs={{0,4},{4,8},{8,12},{12,16},{16,20},{20,24},{24,28},{28,32},{32,36}... | collective-permute-start | bytes 786440 | tf_op jit(solution)/shard_map/while/body/eval_jaxpr/ppermute | solution.py:18
  173.4 10.0 %collective-permute-start.1 = (bf16[256,4,128]{2,0,1:T(8,128)(2,1)}, bf16[256,4,128]{2,0,1:T(8,128)(2,1)S(1)}, u32[]{:S(2)}, u32[]{:S(2)}) collective-permute-start(bf16[256,4,128]{2,0,1:T(8,128)(2,1)} %collective-permute-done), channel_id=1, source_target_pairs={{0,4},{4,8},{8,12},{12,16},{16,20},{20,24},{24,28},{28,32},{32,36}... | collective-permute-start | bytes 786440 | tf_op jit(solution)/shard_map/while/body/eval_jaxpr/ppermute | solution.py:18
  176.2 10.0 %collective-permute-start.3 = (bf16[256,4,128]{2,0,1:T(8,128)(2,1)}, bf16[256,4,128]{2,0,1:T(8,128)(2,1)S(1)}, u32[]{:S(2)}, u32[]{:S(2)}) collective-permute-start(bf16[256,4,128]{2,0,1:T(8,128)(2,1)} %collective-permute-done.2), channel_id=1, source_target_pairs={{0,4},{4,8},{8,12},{12,16},{16,20},{20,24},{24,28},{28,32},{32,36}... | collective-permute-start | bytes 786440 | tf_op jit(solution)/shard_map/while/body/eval_jaxpr/ppermute | solution.py:18
  185.2 1.2 copy-start.5
  186.2 2.8 copy-start.8
  190.0 9.9 %collective-permute-start = (bf16[256,4,128]{2,0,1:T(8,128)(2,1)S(1)}, bf16[256,4,128]{2,0,1:T(8,128)(2,1)}, u32[]{:S(2)}, u32[]{:S(2)}) collective-permute-start(bf16[256,4,128]{2,0,1:T(8,128)(2,1)S(1)} %get-tuple-element.446), channel_id=1, source_target_pairs={{0,4},{4,8},{8,12},{12,16},{16,20},{20,24},{24,28},{28,32},{32,36}... | collective-permute-start | bytes 786440 | tf_op jit(solution)/shard_map/while/body/eval_jaxpr/ppermute | solution.py:18
  191.9 10.8 %collective-permute-start.2 = (bf16[256,4,128]{2,0,1:T(8,128)(2,1)}, bf16[256,4,128]{2,0,1:T(8,128)(2,1)}, u32[]{:S(2)}, u32[]{:S(2)}) collective-permute-start(bf16[256,4,128]{2,0,1:T(8,128)(2,1)} %get-tuple-element.447), channel_id=1, source_target_pairs={{0,4},{4,8},{8,12},{12,16},{16,20},{20,24},{24,28},{28,32},{32,36}... | collective-permute-start | bytes 786440 | tf_op jit(solution)/shard_map/while/body/eval_jaxpr/ppermute | solution.py:18
  199.9 10.0 %collective-permute-start.1 = (bf16[256,4,128]{2,0,1:T(8,128)(2,1)}, bf16[256,4,128]{2,0,1:T(8,128)(2,1)S(1)}, u32[]{:S(2)}, u32[]{:S(2)}) collective-permute-start(bf16[256,4,128]{2,0,1:T(8,128)(2,1)} %collective-permute-done), channel_id=1, source_target_pairs={{0,4},{4,8},{8,12},{12,16},{16,20},{20,24},{24,28},{28,32},{32,36}... | collective-permute-start | bytes 786440 | tf_op jit(solution)/shard_map/while/body/eval_jaxpr/ppermute | solution.py:18
  202.7 10.0 %collective-permute-start.3 = (bf16[256,4,128]{2,0,1:T(8,128)(2,1)}, bf16[256,4,128]{2,0,1:T(8,128)(2,1)S(1)}, u32[]{:S(2)}, u32[]{:S(2)}) collective-permute-start(bf16[256,4,128]{2,0,1:T(8,128)(2,1)} %collective-permute-done.2), channel_id=1, source_target_pairs={{0,4},{4,8},{8,12},{12,16},{16,20},{20,24},{24,28},{28,32},{32,36}... | collective-permute-start | bytes 786440 | tf_op jit(solution)/shard_map/while/body/eval_jaxpr/ppermute | solution.py:18
  211.8 1.2 copy-start.5
  212.7 2.8 copy-start.8
  216.6 9.9 %collective-permute-start = (bf16[256,4,128]{2,0,1:T(8,128)(2,1)S(1)}, bf16[256,4,128]{2,0,1:T(8,128)(2,1)}, u32[]{:S(2)}, u32[]{:S(2)}) collective-permute-start(bf16[256,4,128]{2,0,1:T(8,128)(2,1)S(1)} %get-tuple-element.446), channel_id=1, source_target_pairs={{0,4},{4,8},{8,12},{12,16},{16,20},{20,24},{24,28},{28,32},{32,36}... | collective-permute-start | bytes 786440 | tf_op jit(solution)/shard_map/while/body/eval_jaxpr/ppermute | solution.py:18
  218.5 10.8 %collective-permute-start.2 = (bf16[256,4,128]{2,0,1:T(8,128)(2,1)}, bf16[256,4,128]{2,0,1:T(8,128)(2,1)}, u32[]{:S(2)}, u32[]{:S(2)}) collective-permute-start(bf16[256,4,128]{2,0,1:T(8,128)(2,1)} %get-tuple-element.447), channel_id=1, source_target_pairs={{0,4},{4,8},{8,12},{12,16},{16,20},{20,24},{24,28},{28,32},{32,36}... | collective-permute-start | bytes 786440 | tf_op jit(solution)/shard_map/while/body/eval_jaxpr/ppermute | solution.py:18
  226.5 10.0 %collective-permute-start.1 = (bf16[256,4,128]{2,0,1:T(8,128)(2,1)}, bf16[256,4,128]{2,0,1:T(8,128)(2,1)S(1)}, u32[]{:S(2)}, u32[]{:S(2)}) collective-permute-start(bf16[256,4,128]{2,0,1:T(8,128)(2,1)} %collective-permute-done), channel_id=1, source_target_pairs={{0,4},{4,8},{8,12},{12,16},{16,20},{20,24},{24,28},{28,32},{32,36}... | collective-permute-start | bytes 786440 | tf_op jit(solution)/shard_map/while/body/eval_jaxpr/ppermute | solution.py:18
  229.3 10.0 %collective-permute-start.3 = (bf16[256,4,128]{2,0,1:T(8,128)(2,1)}, bf16[256,4,128]{2,0,1:T(8,128)(2,1)S(1)}, u32[]{:S(2)}, u32[]{:S(2)}) collective-permute-start(bf16[256,4,128]{2,0,1:T(8,128)(2,1)} %collective-permute-done.2), channel_id=1, source_target_pairs={{0,4},{4,8},{8,12},{12,16},{16,20},{20,24},{24,28},{28,32},{32,36}... | collective-permute-start | bytes 786440 | tf_op jit(solution)/shard_map/while/body/eval_jaxpr/ppermute | solution.py:18
  238.3 1.2 copy-start.5
  239.3 2.8 copy-start.8
  247.8 6.6 copy-start.11
  247.8 7.0 %copy-start.13 = (s32[64]{0:T(128)S(1)}, s32[64]{0:T(128)}, u32[]{:S(2)}) copy-start(s32[64]{0:T(128)} %param.26) | copy-start | bytes 772
  252.5 75.4 %copy-start.10 = (f32[2048]{0:T(1024)S(1)}, f32[2048]{0:T(1024)}, u32[]{:S(2)}) copy-start(f32[2048]{0:T(1024)} %param.23) | copy-start | bytes 24580
  324.5 3.4 copy-start.3
  324.5 3.4 copy-start.4
  602.6 4.5 copy-start.12
  602.6 36.3 %all-to-all-start.2 = ((bf16[4,2,163840]{2,1,0:T(2,128)(2,1)}), bf16[4,2,163840]{2,1,0:T(2,128)(2,1)S(1)}, u32[]{:S(2)}, u32[]{:S(2)}) async-start(bf16[4,2,163840]{2,1,0:T(2,128)(2,1)} %reshape.404), calls=%async_computation.2 | async-start | bytes 5242880 | tf_op jit(solution)/shard_map/all_to_all | solution.py:153
  668.3 11.5 %copy-start.1 = (bf16[1,2048,768]{2,1,0:T(8,128)(2,1)S(1)}, bf16[1,2048,768]{2,1,0:T(8,128)(2,1)}, u32[]{:S(2)}) copy-start(bf16[1,2048,768]{2,1,0:T(8,128)(2,1)} %param.29) | copy-start | bytes 9437188
  (6 other events, 6.0 us)
Sparse Core Ops, SparseCore 0:
  10.1 83.0 all-gather.1
  252.6 71.8 all-reduce.1
where the time goes:
time: 696 us; the launch traced here: 687 us
  blocking collectives  208 us (30%)
  waiting for transfers between devices  201 us (29%)
  local copies, waits for them, and re-layouts  105 us (15%)
  starting transfers between devices  67.1 us (10%)
  matrix products  60.8 us (9%)
  other arithmetic  29.8 us (4%)
  between operations  13.9 us (2%)
    all_to_all x1, blocking collectives, per_device(): lax.all_to_all(send_rows, 'req', split_axis=0, concat_axis=0, tiled=True)  106 us
    all_to_all x1, blocking collectives, per_device(): lax.all_to_all(partial_rows[None], 'req', split_axis=1, concat_axis=1, ti...  102 us
    ppermute x32, waiting for transfers between devices, shifted(): lax.ppermute(value, axis, [(source, source + steps) for source in range(i...  99.5 us
    psum x1, waiting for transfers between devices, per_device(): summed = lax.psum(proj.astype(jnp.bfloat16), 'ffn').astype(jnp.float32)  69.6 us
    ppermute x32, starting transfers between devices, shifted(): lax.ppermute(value, axis, [(source, source + steps) for source in range(i...  62.8 us
    all_to_all x1, waiting for transfers between devices, per_device(): lax.all_to_all(lax.all_to_all(partial_rows[None], 'req', split_axis=1, co...  31.6 us
    unnamed x31, local copies, waits for them, and re-layouts  25.2 us
    dot_general x9, matrix products, attend(): jnp.einsum('plyw,wpj->plyj', probs.astype(jnp.bfloat16), values_in_block,...  23.7 us
  transfers between devices with their start and end apart: 35, of which 28 were waited for; matrix products, arithmetic and copies ran while one was open for 10% of the time, Pallas kernels for 0%

commit v1 on v0

--- a/solution.py
+++ b/solution.py
@@ -1,6 +1,8 @@
 import jax
 import jax.numpy as jnp
 from jax import lax
+from jax.experimental import pallas as pl
+from jax.experimental.pallas import tpu as pltpu
 from jax.sharding import PartitionSpec as P
 
 QUERY_HEADS = 32
@@ -20,6 +22,209 @@
 
 def step_back(keys_in_block, values_in_block):
     return shifted((keys_in_block, values_in_block), "req", 1)
+
+
+MESH = pl.DeviceIdType.MESH
+ROW_TILE = 128
+
+
+def greet_group(size):
+    me = lax.axis_index("ffn")
+    barrier = pltpu.get_barrier_semaphore()
+    for d in range(1, size):
+        pl.semaphore_signal(
+            barrier, inc=1, device_id={"ffn": lax.rem(me + d, size)}, device_id_type=MESH
+        )
+    pl.semaphore_wait(barrier, size - 1)
+    return me
+
+
+def send(src, dst, send_sem, recv_sem, peer):
+    copy = pltpu.make_async_remote_copy(
+        src_ref=src,
+        dst_ref=dst,
+        send_sem=send_sem,
+        recv_sem=recv_sem,
+        device_id={"ffn": peer},
+        device_id_type=MESH,
+    )
+    copy.start()
+    return copy
+
+
+def norm_kernel(size, proj_ref, res_ref, gain_ref, hidden_ref, normed_ref, landed, own_sq, peer_sq, s1, r1, s2, r2):
+    width = proj_ref.shape[1]
+    quarter = width // size
+    me = greet_group(size)
+    copies = []
+    for d in range(1, size):
+        peer = lax.rem(me + d, size)
+        cols = pl.ds(pl.multiple_of(peer * quarter, quarter), quarter)
+        copies.append(send(proj_ref.at[:, cols], landed.at[d - 1], s1.at[d - 1], r1.at[d - 1], peer))
+    own = pl.ds(pl.multiple_of(me * quarter, quarter), quarter)
+    hidden_ref[...] = proj_ref[:, own].astype(jnp.float32)
+    for d in (1, 3, 2):
+        copies[d - 1].wait()
+        hidden_ref[...] += landed[d - 1].astype(jnp.float32)
+    hidden = hidden_ref[...] + res_ref[:, own].astype(jnp.float32)
+    hidden_ref[...] = hidden
+    sq = jnp.sum(hidden * hidden, axis=1, keepdims=True)
+    own_sq[...] = jnp.broadcast_to(sq, own_sq.shape)
+    copies = []
+    for d in range(1, size):
+        peer = lax.rem(me + d, size)
+        copies.append(send(own_sq, peer_sq.at[d - 1], s2.at[d - 1], r2.at[d - 1], peer))
+    for copy in copies:
+        copy.wait()
+    total = own_sq[...]
+    for d in range(1, size):
+        total = total + peer_sq[d - 1]
+    scale = lax.rsqrt(total[:, :1] * (1.0 / width) + EPS)
+    normed_ref[...] = (hidden_ref[...] * scale * gain_ref[:, own]).astype(jnp.bfloat16)
+
+
+def norm_call(size, proj, residual, mid_gain):
+    rows, width = proj.shape
+    quarter = width // size
+    vmem = pl.BlockSpec(memory_space=pltpu.VMEM)
+    dma = pltpu.SemaphoreType.DMA((size - 1,))
+    return pl.pallas_call(
+        lambda *refs: norm_kernel(size, *refs),
+        out_shape=(
+            jax.ShapeDtypeStruct((rows, quarter), jnp.float32),
+            jax.ShapeDtypeStruct((rows, quarter), jnp.bfloat16),
+        ),
+        in_specs=[vmem] * 3,
+        out_specs=(vmem, vmem),
+        scratch_shapes=[
+            pltpu.VMEM((size - 1, rows, quarter), jnp.bfloat16),
+            pltpu.VMEM((rows, 128), jnp.float32),
+            pltpu.VMEM((size - 1, rows, 128), jnp.float32),
+            dma,
+            dma,
+            dma,
+            dma,
+        ],
+        compiler_params=pltpu.CompilerParams(collective_id=1, has_side_effects=True),
+        name="norm_exchange",
+    )(proj, residual, mid_gain)
+
+
+def expert_kernel(
+    size, x_ref, gate_hbm, up_hbm, down_hbm, out_ref,
+    gate_mat, up_mat, down_mat, wide, gate_acc, up_acc, act, parts, landed,
+    wsem, s1, r1, s2, r2,
+):
+    rows, quarter = x_ref.shape
+    loads = [
+        pltpu.make_async_copy(gate_hbm, gate_mat, wsem.at[0]),
+        pltpu.make_async_copy(up_hbm, up_mat, wsem.at[1]),
+        pltpu.make_async_copy(down_hbm, down_mat, wsem.at[2]),
+    ]
+    for load in loads:
+        load.start()
+    me = greet_group(size)
+    copies = []
+    for d in range(1, size):
+        peer = lax.rem(me + d, size)
+        copies.append(send(x_ref, wide.at[d - 1], s1.at[d - 1], r1.at[d - 1], peer))
+    loads[0].wait()
+    loads[1].wait()
+    tiles = rows // ROW_TILE
+
+    def tile_rows(tile):
+        return pl.ds(pl.multiple_of(tile * ROW_TILE, ROW_TILE), ROW_TILE)
+
+    for d in (0, 1, 3, 2):
+        if d:
+            copies[d - 1].wait()
+        source = lax.rem(me + size - d, size)
+        k_rows = pl.ds(pl.multiple_of(source * quarter, quarter), quarter)
+
+        def one(tile, carry, d=d, k_rows=k_rows):
+            here = tile_rows(tile)
+            block = x_ref[here, :] if d == 0 else wide[d - 1, here, :]
+            gate = jnp.dot(block, gate_mat[k_rows, :], preferred_element_type=jnp.float32)
+            up = jnp.dot(block, up_mat[k_rows, :], preferred_element_type=jnp.float32)
+            if d == 0:
+                gate_acc[here, :] = gate
+                up_acc[here, :] = up
+            elif d != 2:
+                gate_acc[here, :] += gate
+                up_acc[here, :] += up
+            else:
+                gate = gate_acc[here, :] + gate
+                up = up_acc[here, :] + up
+                act[here, :] = (gate / (1.0 + jnp.exp(-gate)) * up).astype(jnp.bfloat16)
+            return carry
+
+        lax.fori_loop(0, tiles, one, 0)
+    loads[2].wait()
+    copies = {}
+    for d in (2, 1, 3, 0):
+        peer = lax.rem(me + d, size)
+        out_rows = pl.ds(pl.multiple_of(peer * quarter, quarter), quarter)
+
+        def one_part(tile, carry, d=d, out_rows=out_rows):
+            here = tile_rows(tile)
+            part = lax.dot_general(
+                act[here, :],
+                down_mat[out_rows, :],
+                (((1,), (1,)), ((), ())),
+                preferred_element_type=jnp.float32,
+            )
+            parts[d, here, :] = part.astype(jnp.bfloat16)
+            return carry
+
+        lax.fori_loop(0, tiles, one_part, 0)
+        if d:
+            copies[d] = send(parts.at[d], landed.at[d - 1], s2.at[d - 1], r2.at[d - 1], peer)
+    for d in (1, 3, 2):
+        copies[d].wait()
+
+    def total(tile, carry):
+        here = tile_rows(tile)
+        summed = parts[0, here, :].astype(jnp.float32)
+        for d in range(1, size):
+            summed = summed + landed[d - 1, here, :].astype(jnp.float32)
+        out_ref[here, :] = summed.astype(jnp.bfloat16)
+        return carry
+
+    lax.fori_loop(0, tiles, total, 0)
+
+
+def expert_call(size, x, gate_mat, up_mat, down_mat):
+    rows, quarter = x.shape
+    vmem = pl.BlockSpec(memory_space=pltpu.VMEM)
+    hbm = pl.BlockSpec(memory_space=pl.ANY)
+    dma = pltpu.SemaphoreType.DMA((size - 1,))
+    hidden = gate_mat.shape[1]
+    return pl.pallas_call(
+        lambda *refs: expert_kernel(size, *refs),
+        out_shape=jax.ShapeDtypeStruct((rows, quarter), jnp.bfloat16),
+        in_specs=[vmem, hbm, hbm, hbm],
+        out_specs=vmem,
+        scratch_shapes=[
+            pltpu.VMEM(gate_mat.shape, jnp.bfloat16),
+            pltpu.VMEM(up_mat.shape, jnp.bfloat16),
+            pltpu.VMEM(down_mat.shape, jnp.bfloat16),
+            pltpu.VMEM((size - 1, rows, quarter), jnp.bfloat16),
+            pltpu.VMEM((rows, hidden), jnp.float32),
+            pltpu.VMEM((rows, hidden), jnp.float32),
+            pltpu.VMEM((rows, hidden), jnp.bfloat16),
+            pltpu.VMEM((size, rows, quarter), jnp.bfloat16),
+            pltpu.VMEM((size - 1, rows, quarter), jnp.bfloat16),
+            pltpu.SemaphoreType.DMA((3,)),
+            dma,
+            dma,
+            dma,
+            dma,
+        ],
+        compiler_params=pltpu.CompilerParams(
+            collective_id=2, has_side_effects=True, vmem_limit_bytes=40 * 1024 * 1024
+        ),
+        name="expert_exchange",
+    )(x, gate_mat, up_mat, down_mat)
 
 
 def per_device(
@@ -43,7 +248,6 @@
     req_size = lax.axis_size("req")
     ffn_size = lax.axis_size("ffn")
     own_req = lax.axis_index("req")
-    own_ffn = lax.axis_index("ffn")
     query_group_width = QUERY_HEADS // KEY_VALUE_HEADS
     kv_heads = rotated_key_rows.shape[1] // HEAD_SIZE
     quarter = model_width // ffn_size
@@ -121,43 +325,43 @@
         lax.all_gather(out_proj, "req", axis=1, tiled=True),
         preferred_element_type=jnp.float32,
     )
-    summed = lax.psum(proj.astype(jnp.bfloat16), "ffn").astype(jnp.float32)
-    hidden_state = residual.astype(jnp.float32) + summed
-    mean_sq = jnp.mean(hidden_state * hidden_state, axis=1, keepdims=True)
-    normed = (hidden_state * lax.rsqrt(mean_sq + EPS) * mid_gain).astype(jnp.bfloat16)
-    own_hidden = lax.dynamic_slice_in_dim(hidden_state, own_ffn * quarter, quarter, 1)
+    own_hidden, normed = norm_call(
+        ffn_size, proj.astype(jnp.bfloat16), residual, mid_gain.reshape(1, model_width)
+    )
     capacity = 5 * tok_count // (2 * req_size)
     flat_routes = routes.reshape(-1)
     slot_iota = jnp.arange(req_size, dtype=jnp.int32)
     dest_hot = (flat_routes[:, None] == slot_iota[None, :]).astype(jnp.int32)
     slot_depth = jnp.sum((jnp.cumsum(dest_hot, axis=0) - dest_hot) * dest_hot, axis=1)
     slot_index = flat_routes * capacity + slot_depth
-    row_tokens = jnp.arange(2 * tok_count, dtype=jnp.int32) // 2
-    send_rows = (
-        jnp.zeros((req_size * capacity, model_width), jnp.bfloat16)
-        .at[slot_index]
-        .set(normed[row_tokens])
-    )
-    send_rows = send_rows.reshape(req_size, capacity, model_width)
-    arrived = lax.all_to_all(send_rows, "req", split_axis=0, concat_axis=0, tiled=True)
-    flat_rows = arrived.reshape(-1, model_width)
-    gate_val = jnp.dot(flat_rows, gate_mat, preferred_element_type=jnp.float32)
-    up_val = jnp.dot(flat_rows, up_mat, preferred_element_type=jnp.float32)
-    activated = (jax.nn.silu(gate_val) * up_val).astype(jnp.bfloat16)
-    partial_out = lax.dot_general(
-        activated, down_mat, (((1,), (1,)), ((), ())), preferred_element_type=jnp.float32
-    )
-    partial_rows = partial_out.astype(jnp.bfloat16).reshape(
-        arrived.shape[0], arrived.shape[1], model_width
-    )
-    returned_parts = lax.all_to_all(
-        lax.all_to_all(partial_rows[None], "req", split_axis=1, concat_axis=1, tiled=True),
-        "ffn",
-        split_axis=3,
+    slot_pair = slot_index.reshape(tok_count, 2)
+    slots = jnp.arange(req_size * capacity, dtype=jnp.int32)
+    hot_slots = [
+        (slot_pair[:, c][:, None] == slots[None, :]).astype(jnp.bfloat16) for c in range(2)
+    ]
+    send_rows = lax.dot_general(
+        hot_slots[0] + hot_slots[1],
+        normed,
+        (((0,), (0,)), ((), ())),
+        preferred_element_type=jnp.float32,
+    ).astype(jnp.bfloat16)
+    arrived = lax.all_to_all(
+        send_rows.reshape(req_size, capacity, quarter),
+        "req",
+        split_axis=0,
         concat_axis=0,
         tiled=True,
     )
-    returned = jnp.sum(returned_parts.astype(jnp.float32), axis=0)
+    summed_rows = expert_call(
+        ffn_size, arrived.reshape(-1, quarter), gate_mat, up_mat, down_mat
+    )
+    returned = lax.all_to_all(
+        summed_rows.reshape(req_size, capacity, quarter),
+        "req",
+        split_axis=0,
+        concat_axis=0,
+        tiled=True,
+    ).reshape(req_size * capacity, quarter)
     expert_of = jnp.sum(dest_hot * placement[None, :], axis=1).reshape(tok_count, 2)
     expert_hot = (
         expert_of[:, :, None] == jnp.arange(EXPERTS, dtype=jnp.int32)[None, None, :]
@@ -166,10 +370,11 @@
     logit_peak = jnp.max(chosen, axis=1, keepdims=True)
     exp_logits = jnp.exp(chosen - logit_peak)
     gate_weights = exp_logits / jnp.sum(exp_logits, axis=1, keepdims=True)
-    picked = returned.reshape(req_size * capacity, quarter)[slot_index].reshape(
-        tok_count, 2, quarter
-    )
-    mixture = jnp.sum(picked * gate_weights[:, :, None], axis=1)
+    mixture = sum(
+        jnp.dot(hot_slots[c], returned, preferred_element_type=jnp.float32)
+        * gate_weights[:, c][:, None]
+        for c in range(2)
+    )
     return (own_hidden + mixture).astype(jnp.bfloat16)
 
 

time: 696 us -> 434 us (0.62)
  blocking collectives: 208 us -> 56.4 us
  Pallas kernels: 0 us -> 93 us
  local copies, waits for them, and re-layouts: 105 us -> 21.4 us
  waiting for transfers between devices: 201 us -> 128 us
  matrix products: 60.8 us -> 37.4 us
  other arithmetic: 29.8 us -> 11.9 us
    all_to_all x2 -> x1, blocking collectives: 208 us -> 56.4 us  [per_device(): lax.all_to_all(send_rows.reshape(req_size, capacity, quarter), 'req', spl...]
    pallas_call x0 -> x2, Pallas kernels: none -> 93 us  [the longest x1 68.9 us: expert_call(): pl.pallas_call(lambda *refs: expert_kernel(size, *refs), out_shape=jax.Sh...]
    psum x1 -> x0, waiting for transfers between devices: 69.6 us -> none  [per_device(): summed = lax.psum(proj.astype(jnp.bfloat16), 'ffn').astype(jnp.float32)]
    all_to_all x2 -> x0, local copies, waits for them, and re-layouts: 22.2 us -> none  [the longest x1 14.3 us: per_device(): lax.all_to_all(partial_rows[None], 'req', split_axis=1, concat_axis=1, ti...]
    unnamed x31 -> x27, local copies, waits for them, and re-layouts: 25.2 us -> 12.7 us
    dot_general x2 -> x3, matrix products: 15.9 us -> 3.85 us  [the longest x1 2.32 us: per_device(): lax.dot_general(hot_slots[0] + hot_slots[1], normed, (((0,), (0,)), ((),...]
    scatter x1 -> x0, local copies, waits for them, and re-layouts: 11.3 us -> none  [per_device(): send_rows = jnp.zeros((req_size * capacity, model_width), jnp.bfloat16).a...]
    dot_general x9, matrix products: 23.7 us -> 13.5 us  [attend(): jnp.einsum('plyw,wpj->plyj', probs.astype(jnp.bfloat16), values_in_block,...]
  transfers between devices with their start and end apart: 35 -> 34, of which waited for: 28 -> 28; matrix products, arithmetic and copies ran while one was open for 10% -> 12% of each run, Pallas kernels for 0% -> 0%
where the time goes in v1:
time: 434 us; the launch traced here: 431 us
  waiting for transfers between devices  128 us (29%)
  Pallas kernels  93 us (21%)
  starting transfers between devices  68.6 us (16%)
  blocking collectives  56.4 us (13%)
  matrix products  37.4 us (9%)
  local copies, waits for them, and re-layouts  21.4 us (5%)
  between operations  13.6 us (3%)
  other arithmetic  11.9 us (3%)
    ppermute x32, waiting for transfers between devices, shifted(): lax.ppermute(value, axis, [(source, source + steps) for source in range(i...  99.2 us
    pallas_call x1, Pallas kernels, expert_call(): pl.pallas_call(lambda *refs: expert_kernel(size, *refs), out_shape=jax.Sh...  68.9 us
    ppermute x32, starting transfers between devices, shifted(): lax.ppermute(value, axis, [(source, source + steps) for source in range(i...  62.8 us
    all_to_all x1, blocking collectives, per_device(): lax.all_to_all(send_rows.reshape(req_size, capacity, quarter), 'req', spl...  56.4 us
    all_to_all x1, waiting for transfers between devices, per_device(): lax.all_to_all(summed_rows.reshape(req_size, capacity, quarter), 'req', s...  27.6 us
    pallas_call x1, Pallas kernels, norm_call(): pl.pallas_call(lambda *refs: norm_kernel(size, *refs), out_shape=(jax.Sha...  24.1 us
    dot_general x9, matrix products, attend(): jnp.einsum('veck,uek->ecvu', shard_queries, keys_in_block, preferred_elem...  15.6 us
    dot_general x9, matrix products, attend(): jnp.einsum('plyw,wpj->plyj', probs.astype(jnp.bfloat16), values_in_block,...  13.5 us
  transfers between devices with their start and end apart: 34, of which 28 were waited for; matrix products, arithmetic and copies ran while one was open for 12% of the time, Pallas kernels for 0%

profile of v1, /device:TPU:32, one launch (start us, length us, event | category | flops | bytes accessed | tf_op | source)
XLA Modules:
  0.0 431.0 jit_solution(12542860111994806506)
XLA Ops:
  17.9 200.0 %while.24 = (s32[]{:T(128)}, f32[4,2,256]{2,1,0:T(2,128)S(1)}, f32[4,2,256]{2,1,0:T(2,128)S(1)}, f32[4,2,256,128]{3,2,1,0:T(8,128)S(1)}, bf16[256,4,128]{2,0,1:T...) while((s32[]{:T(128)}, f32[4,2,256]{2,1,0:T(2,128)S(1)}, ...), condition=%wide.region_5.6_spmd.clone, body=%wide.region_2.5_spmd.clone.sunk | while | flops 551817984 | bytes 23207316 | solution.py:317
  17.9 1.9 collective-permute-start
  19.9 3.5 collective-permute-start.2
  23.4 4.6 %collective-permute-done = bf16[256,4,128]{2,0,1:T(8,128)(2,1)S(1)} collective-permute-done((bf16[256,4,128]{2,0,1:T(8,128)(2,1)}, bf16[256,4,128]{2,0,1:T(8,128)(2,1)S(1)}, u32[]{:S(2)}, u32[]{:S(2)}) %collective-permute-start) | collective-permute-done | bytes 262176 | tf_op jit(solution)/shard_map/while/body/eval_jaxpr/ppermute | solution.py:20
  28.0 1.9 collective-permute-start.1
  31.1 1.9 collective-permute-start.3
  33.0 5.0 %collective-permute-done.1 = bf16[256,4,128]{2,0,1:T(8,128)(2,1)S(1)} collective-permute-done((bf16[256,4,128]{2,0,1:T(8,128)(2,1)S(1)}, bf16[256,4,128]{2,0,1:T(8,128)(2,1)S(1)}, u32[]{:S(2)}, u32[]{:S(2)}) %collective-permute-start.1) | collective-permute-done | bytes 262176 | tf_op jit(solution)/shard_map/while/body/eval_jaxpr/ppermute | solution.py:20
  38.0 1.9 fusion.70
  42.8 1.9 collective-permute-start
  44.7 1.9 collective-permute-start.2
  46.7 6.3 %collective-permute-done = bf16[256,4,128]{2,0,1:T(8,128)(2,1)S(1)} collective-permute-done((bf16[256,4,128]{2,0,1:T(8,128)(2,1)}, bf16[256,4,128]{2,0,1:T(8,128)(2,1)S(1)}, u32[]{:S(2)}, u32[]{:S(2)}) %collective-permute-start) | collective-permute-done | bytes 262176 | tf_op jit(solution)/shard_map/while/body/eval_jaxpr/ppermute | solution.py:20
  53.0 1.9 collective-permute-start.1
  55.8 1.9 collective-permute-start.3
  57.7 5.1 %collective-permute-done.1 = bf16[256,4,128]{2,0,1:T(8,128)(2,1)S(1)} collective-permute-done((bf16[256,4,128]{2,0,1:T(8,128)(2,1)S(1)}, bf16[256,4,128]{2,0,1:T(8,128)(2,1)S(1)}, u32[]{:S(2)}, u32[]{:S(2)}) %collective-permute-start.1) | collective-permute-done | bytes 262176 | tf_op jit(solution)/shard_map/while/body/eval_jaxpr/ppermute | solution.py:20
  62.7 1.9 fusion.70
  68.4 1.9 collective-permute-start
  70.4 1.9 collective-permute-start.2
  72.3 8.0 %collective-permute-done = bf16[256,4,128]{2,0,1:T(8,128)(2,1)S(1)} collective-permute-done((bf16[256,4,128]{2,0,1:T(8,128)(2,1)}, bf16[256,4,128]{2,0,1:T(8,128)(2,1)S(1)}, u32[]{:S(2)}, u32[]{:S(2)}) %collective-permute-start) | collective-permute-done | bytes 262176 | tf_op jit(solution)/shard_map/while/body/eval_jaxpr/ppermute | solution.py:20
  80.3 1.9 collective-permute-start.1
  82.5 2.8 collective-permute-done.2
  85.3 1.9 collective-permute-start.3
  87.2 3.5 collective-permute-done.1
  90.7 1.9 fusion.70
  96.7 1.9 collective-permute-start
  98.6 1.9 collective-permute-start.2
  100.5 6.1 %collective-permute-done = bf16[256,4,128]{2,0,1:T(8,128)(2,1)S(1)} collective-permute-done((bf16[256,4,128]{2,0,1:T(8,128)(2,1)}, bf16[256,4,128]{2,0,1:T(8,128)(2,1)S(1)}, u32[]{:S(2)}, u32[]{:S(2)}) %collective-permute-start) | collective-permute-done | bytes 262176 | tf_op jit(solution)/shard_map/while/body/eval_jaxpr/ppermute | solution.py:20
  106.7 1.9 collective-permute-start.1
  109.5 1.9 collective-permute-start.3
  111.4 5.1 %collective-permute-done.1 = bf16[256,4,128]{2,0,1:T(8,128)(2,1)S(1)} collective-permute-done((bf16[256,4,128]{2,0,1:T(8,128)(2,1)S(1)}, bf16[256,4,128]{2,0,1:T(8,128)(2,1)S(1)}, u32[]{:S(2)}, u32[]{:S(2)}) %collective-permute-start.1) | collective-permute-done | bytes 262176 | tf_op jit(solution)/shard_map/while/body/eval_jaxpr/ppermute | solution.py:20
  120.9 1.9 collective-permute-start
  122.9 1.9 collective-permute-start.2
  124.8 6.1 %collective-permute-done = bf16[256,4,128]{2,0,1:T(8,128)(2,1)S(1)} collective-permute-done((bf16[256,4,128]{2,0,1:T(8,128)(2,1)}, bf16[256,4,128]{2,0,1:T(8,128)(2,1)S(1)}, u32[]{:S(2)}, u32[]{:S(2)}) %collective-permute-start) | collective-permute-done | bytes 262176 | tf_op jit(solution)/shard_map/while/body/eval_jaxpr/ppermute | solution.py:20
  130.9 1.9 collective-permute-start.1
  133.7 1.9 collective-permute-start.3
  135.7 5.1 %collective-permute-done.1 = bf16[256,4,128]{2,0,1:T(8,128)(2,1)S(1)} collective-permute-done((bf16[256,4,128]{2,0,1:T(8,128)(2,1)S(1)}, bf16[256,4,128]{2,0,1:T(8,128)(2,1)S(1)}, u32[]{:S(2)}, u32[]{:S(2)}) %collective-permute-start.1) | collective-permute-done | bytes 262176 | tf_op jit(solution)/shard_map/while/body/eval_jaxpr/ppermute | solution.py:20
  140.7 1.9 fusion.70
  145.2 1.9 collective-permute-start
  147.1 1.9 collective-permute-start.2
  149.1 6.1 %collective-permute-done = bf16[256,4,128]{2,0,1:T(8,128)(2,1)S(1)} collective-permute-done((bf16[256,4,128]{2,0,1:T(8,128)(2,1)}, bf16[256,4,128]{2,0,1:T(8,128)(2,1)S(1)}, u32[]{:S(2)}, u32[]{:S(2)}) %collective-permute-start) | collective-permute-done | bytes 262176 | tf_op jit(solution)/shard_map/while/body/eval_jaxpr/ppermute | solution.py:20
  155.2 1.9 collective-permute-start.1
  158.0 1.9 collective-permute-start.3
  159.9 5.1 %collective-permute-done.1 = bf16[256,4,128]{2,0,1:T(8,128)(2,1)S(1)} collective-permute-done((bf16[256,4,128]{2,0,1:T(8,128)(2,1)S(1)}, bf16[256,4,128]{2,0,1:T(8,128)(2,1)S(1)}, u32[]{:S(2)}, u32[]{:S(2)}) %collective-permute-start.1) | collective-permute-done | bytes 262176 | tf_op jit(solution)/shard_map/while/body/eval_jaxpr/ppermute | solution.py:20
  169.4 1.9 collective-permute-start
  171.4 1.9 collective-permute-start.2
  173.3 6.1 %collective-permute-done = bf16[256,4,128]{2,0,1:T(8,128)(2,1)S(1)} collective-permute-done((bf16[256,4,128]{2,0,1:T(8,128)(2,1)}, bf16[256,4,128]{2,0,1:T(8,128)(2,1)S(1)}, u32[]{:S(2)}, u32[]{:S(2)}) %collective-permute-start) | collective-permute-done | bytes 262176 | tf_op jit(solution)/shard_map/while/body/eval_jaxpr/ppermute | solution.py:20
  179.5 1.9 collective-permute-start.1
  182.3 1.9 collective-permute-start.3
  184.2 5.1 %collective-permute-done.1 = bf16[256,4,128]{2,0,1:T(8,128)(2,1)S(1)} collective-permute-done((bf16[256,4,128]{2,0,1:T(8,128)(2,1)S(1)}, bf16[256,4,128]{2,0,1:T(8,128)(2,1)S(1)}, u32[]{:S(2)}, u32[]{:S(2)}) %collective-permute-start.1) | collective-permute-done | bytes 262176 | tf_op jit(solution)/shard_map/while/body/eval_jaxpr/ppermute | solution.py:20
  193.7 1.9 collective-permute-start
  195.6 1.9 collective-permute-start.2
  197.6 6.1 %collective-permute-done = bf16[256,4,128]{2,0,1:T(8,128)(2,1)S(1)} collective-permute-done((bf16[256,4,128]{2,0,1:T(8,128)(2,1)}, bf16[256,4,128]{2,0,1:T(8,128)(2,1)S(1)}, u32[]{:S(2)}, u32[]{:S(2)}) %collective-permute-start) | collective-permute-done | bytes 262176 | tf_op jit(solution)/shard_map/while/body/eval_jaxpr/ppermute | solution.py:20
  203.7 1.9 collective-permute-start.1
  206.5 1.9 collective-permute-start.3
  208.4 5.1 %collective-permute-done.1 = bf16[256,4,128]{2,0,1:T(8,128)(2,1)S(1)} collective-permute-done((bf16[256,4,128]{2,0,1:T(8,128)(2,1)S(1)}, bf16[256,4,128]{2,0,1:T(8,128)(2,1)S(1)}, u32[]{:S(2)}, u32[]{:S(2)}) %collective-permute-start.1) | collective-permute-done | bytes 262176 | tf_op jit(solution)/shard_map/while/body/eval_jaxpr/ppermute | solution.py:20
  220.3 4.5 %convolution_convert_fusion.refs_0_ = bf16[256,2048]{1,0:T(8,128)(2,1)} fusion(bf16[256,1024]{0,1:T(8,128)(2,1)S(1)} %bitcast.117, bf16[1024,2048]{0,1:T(8,128)(2,1)} %all-gather.2.cloned.1.call-done), kind=kOutput, calls=%fused_computation.29 | convolution fusion | flops 1074266112 | bytes 5767168 | tf_op jit(solution)/shard_map/dot_general | solution.py:323
  224.8 24.1 %norm_exchange.1 = (f32[256,512]{1,0:T(8,128)}, bf16[256,512]{1,0:T(8,128)(2,1)}) custom-call(bf16[256,2048]{1,0:T(8,128)(2,1)} %convolution_convert_fusion.refs_0_, bf16[256,2048]{1,0:T(8,128)(2,1)} %refs_1_.1, f32[1,2048]{1,0:T(1,128)} %bitcast.121), custom_call_target="tpu_custom_call" | custom-call | tf_op jit(solution)/shard_map/norm_exchange/pallas_call | solution.py:91
  248.9 2.3 convolution_convert_fusion.1
  251.2 2.1 reshape.253
  253.4 56.4 %all_to_all.10 = bf16[64,10,512]{2,1,0:T(8,128)(2,1)} all-to-all(bf16[64,10,512]{2,1,0:T(8,128)(2,1)} %reshape.253), channel_id=1, replica_groups=mesh['req'=64,'ffn'=4] {'req'}, dimensions={0} | all-to-all | bytes 1310720 | tf_op jit(solution)/shard_map/all_to_all | solution.py:348
  309.8 2.1 reshape.254.refs_0_
  316.7 68.9 %expert_exchange.1 = bf16[640,512]{1,0:T(8,128)(2,1)S(1)} custom-call(bf16[640,512]{1,0:T(8,128)(2,1)S(1)} %copy-done.3, bf16[2048,768]{1,0:T(8,128)(2,1)S(1)} %bitcast.105, bf16[2048,768]{1,0:T(8,128)(2,1)S(1)} %bitcast.106, bf16[2048,768]{1,0:T(8,128)(2,1)S(1)} %bitcast.107), custom_call_target="tpu_custom_call" | custom-call | tf_op jit(solution)/shard_map/expert_exchange/pallas_call | solution.py:202
  386.5 2.2 reshape.255
  388.7 5.8 %all-to-all-start.1 = ((bf16[64,10,512]{2,1,0:T(8,128)(2,1)}), bf16[64,10,512]{2,1,0:T(8,128)(2,1)S(1)}, u32[]{:S(2)}, u32[]{:S(2)}) async-start(bf16[64,10,512]{2,1,0:T(8,128)(2,1)} %reshape.255), calls=%async_computation.1 | async-start | bytes 2097152 | tf_op jit(solution)/shard_map/all_to_all | solution.py:358
  394.8 27.6 %all-to-all-done.1 = bf16[64,10,512]{2,1,0:T(8,128)(2,1)S(1)} async-done(((bf16[64,10,512]{2,1,0:T(8,128)(2,1)}), bf16[64,10,512]{2,1,0:T(8,128)(2,1)S(1)}, u32[]{:S(2)}, u32[]{:S(2)}) %all-to-all-start.1) | async-done | bytes 655392 | tf_op jit(solution)/shard_map/all_to_all | solution.py:358
  (177 shorter events, 58.7 us)
Async XLA Ops:
  6.5 213.8 %all-gather.2.cloned.1.call-start = ((), (), s32[]{:S(2)}) async-start(), calls=%async_computation.2 | async-start | bytes 4259840 | tf_op jit(solution)/shard_map/all_gather | solution.py:325
  13.8 4.1 copy-start.8
  17.9 201.9 %copy-start.11 = (s32[64]{0:T(128)S(1)}, s32[64]{0:T(128)}, u32[]{:S(2)}) copy-start(s32[64]{0:T(128)} %param.26) | copy-start | bytes 772
  17.9 202.2 %copy-start.9 = (s32[256,2]{0,1:T(2,128)S(1)}, s32[256,2]{0,1:T(2,128)}, u32[]{:S(2)}) copy-start(s32[256,2]{0,1:T(2,128)} %param.25) | copy-start | bytes 6148
  17.9 10.0 %collective-permute-start = (bf16[256,4,128]{2,0,1:T(8,128)(2,1)}, bf16[256,4,128]{2,0,1:T(8,128)(2,1)S(1)}, u32[]{:S(2)}, u32[]{:S(2)}) collective-permute-start(bf16[256,4,128]{2,0,1:T(8,128)(2,1)} %get-tuple-element.442), channel_id=1, source_target_pairs={{0,4},{4,8},{8,12},{12,16},{16,20},{20,24},{24,28},{28,32},{32,36}... | collective-permute-start | bytes 786440 | tf_op jit(solution)/shard_map/while/body/eval_jaxpr/ppermute | solution.py:20
  19.9 11.2 %collective-permute-start.2 = (bf16[256,4,128]{2,0,1:T(8,128)(2,1)}, bf16[256,4,128]{2,0,1:T(8,128)(2,1)S(1)}, u32[]{:S(2)}, u32[]{:S(2)}) collective-permute-start(bf16[256,4,128]{2,0,1:T(8,128)(2,1)} %get-tuple-element.443), channel_id=1, source_target_pairs={{0,4},{4,8},{8,12},{12,16},{16,20},{20,24},{24,28},{28,32},{32,36}... | collective-permute-start | bytes 786440 | tf_op jit(solution)/shard_map/while/body/eval_jaxpr/ppermute | solution.py:20
  28.0 10.1 %collective-permute-start.1 = (bf16[256,4,128]{2,0,1:T(8,128)(2,1)S(1)}, bf16[256,4,128]{2,0,1:T(8,128)(2,1)S(1)}, u32[]{:S(2)}, u32[]{:S(2)}) collective-permute-start(bf16[256,4,128]{2,0,1:T(8,128)(2,1)S(1)} %collective-permute-done), channel_id=1, source_target_pairs={{0,4},{4,8},{8,12},{12,16},{16,20},{20,24},{24,28},{28,32},{32,36}... | collective-permute-start | bytes 786440 | tf_op jit(solution)/shard_map/while/body/eval_jaxpr/ppermute | solution.py:20
  31.1 10.1 %collective-permute-start.3 = (bf16[256,4,128]{2,0,1:T(8,128)(2,1)S(1)}, bf16[256,4,128]{2,0,1:T(8,128)(2,1)S(1)}, u32[]{:S(2)}, u32[]{:S(2)}) collective-permute-start(bf16[256,4,128]{2,0,1:T(8,128)(2,1)S(1)} %collective-permute-done.2), channel_id=1, source_target_pairs={{0,4},{4,8},{8,12},{12,16},{16,20},{20,24},{24,28},{28,32},{32,36}... | collective-permute-start | bytes 786440 | tf_op jit(solution)/shard_map/while/body/eval_jaxpr/ppermute | solution.py:20
  38.0 2.8 copy-start.6
  41.2 1.6 copy-start.7
  42.8 10.1 %collective-permute-start = (bf16[256,4,128]{2,0,1:T(8,128)(2,1)}, bf16[256,4,128]{2,0,1:T(8,128)(2,1)S(1)}, u32[]{:S(2)}, u32[]{:S(2)}) collective-permute-start(bf16[256,4,128]{2,0,1:T(8,128)(2,1)} %get-tuple-element.442), channel_id=1, source_target_pairs={{0,4},{4,8},{8,12},{12,16},{16,20},{20,24},{24,28},{28,32},{32,36}... | collective-permute-start | bytes 786440 | tf_op jit(solution)/shard_map/while/body/eval_jaxpr/ppermute | solution.py:20
  44.7 11.0 %collective-permute-start.2 = (bf16[256,4,128]{2,0,1:T(8,128)(2,1)}, bf16[256,4,128]{2,0,1:T(8,128)(2,1)S(1)}, u32[]{:S(2)}, u32[]{:S(2)}) collective-permute-start(bf16[256,4,128]{2,0,1:T(8,128)(2,1)} %get-tuple-element.443), channel_id=1, source_target_pairs={{0,4},{4,8},{8,12},{12,16},{16,20},{20,24},{24,28},{28,32},{32,36}... | collective-permute-start | bytes 786440 | tf_op jit(solution)/shard_map/while/body/eval_jaxpr/ppermute | solution.py:20
  53.0 9.8 %collective-permute-start.1 = (bf16[256,4,128]{2,0,1:T(8,128)(2,1)S(1)}, bf16[256,4,128]{2,0,1:T(8,128)(2,1)S(1)}, u32[]{:S(2)}, u32[]{:S(2)}) collective-permute-start(bf16[256,4,128]{2,0,1:T(8,128)(2,1)S(1)} %collective-permute-done), channel_id=1, source_target_pairs={{0,4},{4,8},{8,12},{12,16},{16,20},{20,24},{24,28},{28,32},{32,36}... | collective-permute-start | bytes 786440 | tf_op jit(solution)/shard_map/while/body/eval_jaxpr/ppermute | solution.py:20
  55.8 11.1 %collective-permute-start.3 = (bf16[256,4,128]{2,0,1:T(8,128)(2,1)S(1)}, bf16[256,4,128]{2,0,1:T(8,128)(2,1)S(1)}, u32[]{:S(2)}, u32[]{:S(2)}) collective-permute-start(bf16[256,4,128]{2,0,1:T(8,128)(2,1)S(1)} %collective-permute-done.2), channel_id=1, source_target_pairs={{0,4},{4,8},{8,12},{12,16},{16,20},{20,24},{24,28},{28,32},{32,36}... | collective-permute-start | bytes 786440 | tf_op jit(solution)/shard_map/while/body/eval_jaxpr/ppermute | solution.py:20
  62.7 2.8 copy-start.6
  66.8 1.6 copy-start.7
  68.4 11.9 %collective-permute-start = (bf16[256,4,128]{2,0,1:T(8,128)(2,1)}, bf16[256,4,128]{2,0,1:T(8,128)(2,1)S(1)}, u32[]{:S(2)}, u32[]{:S(2)}) collective-permute-start(bf16[256,4,128]{2,0,1:T(8,128)(2,1)} %get-tuple-element.442), channel_id=1, source_target_pairs={{0,4},{4,8},{8,12},{12,16},{16,20},{20,24},{24,28},{28,32},{32,36}... | collective-permute-start | bytes 786440 | tf_op jit(solution)/shard_map/while/body/eval_jaxpr/ppermute | solution.py:20
  70.4 14.9 %collective-permute-start.2 = (bf16[256,4,128]{2,0,1:T(8,128)(2,1)}, bf16[256,4,128]{2,0,1:T(8,128)(2,1)S(1)}, u32[]{:S(2)}, u32[]{:S(2)}) collective-permute-start(bf16[256,4,128]{2,0,1:T(8,128)(2,1)} %get-tuple-element.443), channel_id=1, source_target_pairs={{0,4},{4,8},{8,12},{12,16},{16,20},{20,24},{24,28},{28,32},{32,36}... | collective-permute-start | bytes 786440 | tf_op jit(solution)/shard_map/while/body/eval_jaxpr/ppermute | solution.py:20
  80.3 10.3 %collective-permute-start.1 = (bf16[256,4,128]{2,0,1:T(8,128)(2,1)S(1)}, bf16[256,4,128]{2,0,1:T(8,128)(2,1)S(1)}, u32[]{:S(2)}, u32[]{:S(2)}) collective-permute-start(bf16[256,4,128]{2,0,1:T(8,128)(2,1)S(1)} %collective-permute-done), channel_id=1, source_target_pairs={{0,4},{4,8},{8,12},{12,16},{16,20},{20,24},{24,28},{28,32},{32,36}... | collective-permute-start | bytes 786440 | tf_op jit(solution)/shard_map/while/body/eval_jaxpr/ppermute | solution.py:20
  85.3 9.8 %collective-permute-start.3 = (bf16[256,4,128]{2,0,1:T(8,128)(2,1)S(1)}, bf16[256,4,128]{2,0,1:T(8,128)(2,1)S(1)}, u32[]{:S(2)}, u32[]{:S(2)}) collective-permute-start(bf16[256,4,128]{2,0,1:T(8,128)(2,1)S(1)} %collective-permute-done.2), channel_id=1, source_target_pairs={{0,4},{4,8},{8,12},{12,16},{16,20},{20,24},{24,28},{28,32},{32,36}... | collective-permute-start | bytes 786440 | tf_op jit(solution)/shard_map/while/body/eval_jaxpr/ppermute | solution.py:20
  90.7 2.8 copy-start.6
  95.1 1.6 copy-start.7
  96.7 10.0 %collective-permute-start = (bf16[256,4,128]{2,0,1:T(8,128)(2,1)}, bf16[256,4,128]{2,0,1:T(8,128)(2,1)S(1)}, u32[]{:S(2)}, u32[]{:S(2)}) collective-permute-start(bf16[256,4,128]{2,0,1:T(8,128)(2,1)} %get-tuple-element.442), channel_id=1, source_target_pairs={{0,4},{4,8},{8,12},{12,16},{16,20},{20,24},{24,28},{28,32},{32,36}... | collective-permute-start | bytes 786440 | tf_op jit(solution)/shard_map/while/body/eval_jaxpr/ppermute | solution.py:20
  98.6 10.9 %collective-permute-start.2 = (bf16[256,4,128]{2,0,1:T(8,128)(2,1)}, bf16[256,4,128]{2,0,1:T(8,128)(2,1)S(1)}, u32[]{:S(2)}, u32[]{:S(2)}) collective-permute-start(bf16[256,4,128]{2,0,1:T(8,128)(2,1)} %get-tuple-element.443), channel_id=1, source_target_pairs={{0,4},{4,8},{8,12},{12,16},{16,20},{20,24},{24,28},{28,32},{32,36}... | collective-permute-start | bytes 786440 | tf_op jit(solution)/shard_map/while/body/eval_jaxpr/ppermute | solution.py:20
  106.7 9.8 %collective-permute-start.1 = (bf16[256,4,128]{2,0,1:T(8,128)(2,1)S(1)}, bf16[256,4,128]{2,0,1:T(8,128)(2,1)S(1)}, u32[]{:S(2)}, u32[]{:S(2)}) collective-permute-start(bf16[256,4,128]{2,0,1:T(8,128)(2,1)S(1)} %collective-permute-done), channel_id=1, source_target_pairs={{0,4},{4,8},{8,12},{12,16},{16,20},{20,24},{24,28},{28,32},{32,36}... | collective-permute-start | bytes 786440 | tf_op jit(solution)/shard_map/while/body/eval_jaxpr/ppermute | solution.py:20
  109.5 9.8 %collective-permute-start.3 = (bf16[256,4,128]{2,0,1:T(8,128)(2,1)S(1)}, bf16[256,4,128]{2,0,1:T(8,128)(2,1)S(1)}, u32[]{:S(2)}, u32[]{:S(2)}) collective-permute-start(bf16[256,4,128]{2,0,1:T(8,128)(2,1)S(1)} %collective-permute-done.2), channel_id=1, source_target_pairs={{0,4},{4,8},{8,12},{12,16},{16,20},{20,24},{24,28},{28,32},{32,36}... | collective-permute-start | bytes 786440 | tf_op jit(solution)/shard_map/while/body/eval_jaxpr/ppermute | solution.py:20
  116.5 2.8 copy-start.6
  119.3 1.6 copy-start.7
  120.9 10.0 %collective-permute-start = (bf16[256,4,128]{2,0,1:T(8,128)(2,1)}, bf16[256,4,128]{2,0,1:T(8,128)(2,1)S(1)}, u32[]{:S(2)}, u32[]{:S(2)}) collective-permute-start(bf16[256,4,128]{2,0,1:T(8,128)(2,1)} %get-tuple-element.442), channel_id=1, source_target_pairs={{0,4},{4,8},{8,12},{12,16},{16,20},{20,24},{24,28},{28,32},{32,36}... | collective-permute-start | bytes 786440 | tf_op jit(solution)/shard_map/while/body/eval_jaxpr/ppermute | solution.py:20
  122.9 10.9 %collective-permute-start.2 = (bf16[256,4,128]{2,0,1:T(8,128)(2,1)}, bf16[256,4,128]{2,0,1:T(8,128)(2,1)S(1)}, u32[]{:S(2)}, u32[]{:S(2)}) collective-permute-start(bf16[256,4,128]{2,0,1:T(8,128)(2,1)} %get-tuple-element.443), channel_id=1, source_target_pairs={{0,4},{4,8},{8,12},{12,16},{16,20},{20,24},{24,28},{28,32},{32,36}... | collective-permute-start | bytes 786440 | tf_op jit(solution)/shard_map/while/body/eval_jaxpr/ppermute | solution.py:20
  130.9 9.8 %collective-permute-start.1 = (bf16[256,4,128]{2,0,1:T(8,128)(2,1)S(1)}, bf16[256,4,128]{2,0,1:T(8,128)(2,1)S(1)}, u32[]{:S(2)}, u32[]{:S(2)}) collective-permute-start(bf16[256,4,128]{2,0,1:T(8,128)(2,1)S(1)} %collective-permute-done), channel_id=1, source_target_pairs={{0,4},{4,8},{8,12},{12,16},{16,20},{20,24},{24,28},{28,32},{32,36}... | collective-permute-start | bytes 786440 | tf_op jit(solution)/shard_map/while/body/eval_jaxpr/ppermute | solution.py:20
  133.7 9.8 %collective-permute-start.3 = (bf16[256,4,128]{2,0,1:T(8,128)(2,1)S(1)}, bf16[256,4,128]{2,0,1:T(8,128)(2,1)S(1)}, u32[]{:S(2)}, u32[]{:S(2)}) collective-permute-start(bf16[256,4,128]{2,0,1:T(8,128)(2,1)S(1)} %collective-permute-done.2), channel_id=1, source_target_pairs={{0,4},{4,8},{8,12},{12,16},{16,20},{20,24},{24,28},{28,32},{32,36}... | collective-permute-start | bytes 786440 | tf_op jit(solution)/shard_map/while/body/eval_jaxpr/ppermute | solution.py:20
  140.7 2.8 copy-start.6
  143.6 1.6 copy-start.7
  145.2 10.0 %collective-permute-start = (bf16[256,4,128]{2,0,1:T(8,128)(2,1)}, bf16[256,4,128]{2,0,1:T(8,128)(2,1)S(1)}, u32[]{:S(2)}, u32[]{:S(2)}) collective-permute-start(bf16[256,4,128]{2,0,1:T(8,128)(2,1)} %get-tuple-element.442), channel_id=1, source_target_pairs={{0,4},{4,8},{8,12},{12,16},{16,20},{20,24},{24,28},{28,32},{32,36}... | collective-permute-start | bytes 786440 | tf_op jit(solution)/shard_map/while/body/eval_jaxpr/ppermute | solution.py:20
  147.1 10.9 %collective-permute-start.2 = (bf16[256,4,128]{2,0,1:T(8,128)(2,1)}, bf16[256,4,128]{2,0,1:T(8,128)(2,1)S(1)}, u32[]{:S(2)}, u32[]{:S(2)}) collective-permute-start(bf16[256,4,128]{2,0,1:T(8,128)(2,1)} %get-tuple-element.443), channel_id=1, source_target_pairs={{0,4},{4,8},{8,12},{12,16},{16,20},{20,24},{24,28},{28,32},{32,36}... | collective-permute-start | bytes 786440 | tf_op jit(solution)/shard_map/while/body/eval_jaxpr/ppermute | solution.py:20
  155.2 9.8 %collective-permute-start.1 = (bf16[256,4,128]{2,0,1:T(8,128)(2,1)S(1)}, bf16[256,4,128]{2,0,1:T(8,128)(2,1)S(1)}, u32[]{:S(2)}, u32[]{:S(2)}) collective-permute-start(bf16[256,4,128]{2,0,1:T(8,128)(2,1)S(1)} %collective-permute-done), channel_id=1, source_target_pairs={{0,4},{4,8},{8,12},{12,16},{16,20},{20,24},{24,28},{28,32},{32,36}... | collective-permute-start | bytes 786440 | tf_op jit(solution)/shard_map/while/body/eval_jaxpr/ppermute | solution.py:20
  158.0 9.8 %collective-permute-start.3 = (bf16[256,4,128]{2,0,1:T(8,128)(2,1)S(1)}, bf16[256,4,128]{2,0,1:T(8,128)(2,1)S(1)}, u32[]{:S(2)}, u32[]{:S(2)}) collective-permute-start(bf16[256,4,128]{2,0,1:T(8,128)(2,1)S(1)} %collective-permute-done.2), channel_id=1, source_target_pairs={{0,4},{4,8},{8,12},{12,16},{16,20},{20,24},{24,28},{28,32},{32,36}... | collective-permute-start | bytes 786440 | tf_op jit(solution)/shard_map/while/body/eval_jaxpr/ppermute | solution.py:20
  165.0 2.8 copy-start.6
  167.8 1.6 copy-start.7
  169.4 10.0 %collective-permute-start = (bf16[256,4,128]{2,0,1:T(8,128)(2,1)}, bf16[256,4,128]{2,0,1:T(8,128)(2,1)S(1)}, u32[]{:S(2)}, u32[]{:S(2)}) collective-permute-start(bf16[256,4,128]{2,0,1:T(8,128)(2,1)} %get-tuple-element.442), channel_id=1, source_target_pairs={{0,4},{4,8},{8,12},{12,16},{16,20},{20,24},{24,28},{28,32},{32,36}... | collective-permute-start | bytes 786440 | tf_op jit(solution)/shard_map/while/body/eval_jaxpr/ppermute | solution.py:20
  171.4 10.9 %collective-permute-start.2 = (bf16[256,4,128]{2,0,1:T(8,128)(2,1)}, bf16[256,4,128]{2,0,1:T(8,128)(2,1)S(1)}, u32[]{:S(2)}, u32[]{:S(2)}) collective-permute-start(bf16[256,4,128]{2,0,1:T(8,128)(2,1)} %get-tuple-element.443), channel_id=1, source_target_pairs={{0,4},{4,8},{8,12},{12,16},{16,20},{20,24},{24,28},{28,32},{32,36}... | collective-permute-start | bytes 786440 | tf_op jit(solution)/shard_map/while/body/eval_jaxpr/ppermute | solution.py:20
  179.5 9.8 %collective-permute-start.1 = (bf16[256,4,128]{2,0,1:T(8,128)(2,1)S(1)}, bf16[256,4,128]{2,0,1:T(8,128)(2,1)S(1)}, u32[]{:S(2)}, u32[]{:S(2)}) collective-permute-start(bf16[256,4,128]{2,0,1:T(8,128)(2,1)S(1)} %collective-permute-done), channel_id=1, source_target_pairs={{0,4},{4,8},{8,12},{12,16},{16,20},{20,24},{24,28},{28,32},{32,36}... | collective-permute-start | bytes 786440 | tf_op jit(solution)/shard_map/while/body/eval_jaxpr/ppermute | solution.py:20
  182.3 9.8 %collective-permute-start.3 = (bf16[256,4,128]{2,0,1:T(8,128)(2,1)S(1)}, bf16[256,4,128]{2,0,1:T(8,128)(2,1)S(1)}, u32[]{:S(2)}, u32[]{:S(2)}) collective-permute-start(bf16[256,4,128]{2,0,1:T(8,128)(2,1)S(1)} %collective-permute-done.2), channel_id=1, source_target_pairs={{0,4},{4,8},{8,12},{12,16},{16,20},{20,24},{24,28},{28,32},{32,36}... | collective-permute-start | bytes 786440 | tf_op jit(solution)/shard_map/while/body/eval_jaxpr/ppermute | solution.py:20
  189.2 2.8 copy-start.6
  192.1 1.6 copy-start.7
  193.7 10.0 %collective-permute-start = (bf16[256,4,128]{2,0,1:T(8,128)(2,1)}, bf16[256,4,128]{2,0,1:T(8,128)(2,1)S(1)}, u32[]{:S(2)}, u32[]{:S(2)}) collective-permute-start(bf16[256,4,128]{2,0,1:T(8,128)(2,1)} %get-tuple-element.442), channel_id=1, source_target_pairs={{0,4},{4,8},{8,12},{12,16},{16,20},{20,24},{24,28},{28,32},{32,36}... | collective-permute-start | bytes 786440 | tf_op jit(solution)/shard_map/while/body/eval_jaxpr/ppermute | solution.py:20
  195.6 10.9 %collective-permute-start.2 = (bf16[256,4,128]{2,0,1:T(8,128)(2,1)}, bf16[256,4,128]{2,0,1:T(8,128)(2,1)S(1)}, u32[]{:S(2)}, u32[]{:S(2)}) collective-permute-start(bf16[256,4,128]{2,0,1:T(8,128)(2,1)} %get-tuple-element.443), channel_id=1, source_target_pairs={{0,4},{4,8},{8,12},{12,16},{16,20},{20,24},{24,28},{28,32},{32,36}... | collective-permute-start | bytes 786440 | tf_op jit(solution)/shard_map/while/body/eval_jaxpr/ppermute | solution.py:20
  203.7 9.8 %collective-permute-start.1 = (bf16[256,4,128]{2,0,1:T(8,128)(2,1)S(1)}, bf16[256,4,128]{2,0,1:T(8,128)(2,1)S(1)}, u32[]{:S(2)}, u32[]{:S(2)}) collective-permute-start(bf16[256,4,128]{2,0,1:T(8,128)(2,1)S(1)} %collective-permute-done), channel_id=1, source_target_pairs={{0,4},{4,8},{8,12},{12,16},{16,20},{20,24},{24,28},{28,32},{32,36}... | collective-permute-start | bytes 786440 | tf_op jit(solution)/shard_map/while/body/eval_jaxpr/ppermute | solution.py:20
  206.5 9.8 %collective-permute-start.3 = (bf16[256,4,128]{2,0,1:T(8,128)(2,1)S(1)}, bf16[256,4,128]{2,0,1:T(8,128)(2,1)S(1)}, u32[]{:S(2)}, u32[]{:S(2)}) collective-permute-start(bf16[256,4,128]{2,0,1:T(8,128)(2,1)S(1)} %collective-permute-done.2), channel_id=1, source_target_pairs={{0,4},{4,8},{8,12},{12,16},{16,20},{20,24},{24,28},{28,32},{32,36}... | collective-permute-start | bytes 786440 | tf_op jit(solution)/shard_map/while/body/eval_jaxpr/ppermute | solution.py:20
  213.5 2.8 copy-start.6
  216.3 1.6 copy-start.7
  224.8 87.1 %copy-start = (bf16[1,2048,768]{2,1,0:T(8,128)(2,1)S(1)}, bf16[1,2048,768]{2,1,0:T(8,128)(2,1)}, u32[]{:S(2)}) copy-start(bf16[1,2048,768]{2,1,0:T(8,128)(2,1)} %param.27) | copy-start | bytes 9437188
  311.9 1.9 copy-start.1
  313.8 1.9 copy-start.2
  315.6 1.1 copy-start.3
  316.7 77.9 %copy-start.10 = (f32[256,8]{0,1:T(8,128)S(1)}, f32[256,8]{0,1:T(8,128)}, u32[]{:S(2)}) copy-start(f32[256,8]{0,1:T(8,128)} %param.24) | copy-start | bytes 24580
  385.6 0.9 copy-start.4
  386.5 36.5 %copy-start.5 = (f32[256,512]{1,0:T(8,128)S(1)}, f32[256,512]{1,0:T(8,128)}, u32[]{:S(2)}) copy-start(f32[256,512]{1,0:T(8,128)} %get-tuple-element.252) | copy-start | bytes 1572868
  388.7 33.7 %all-to-all-start.1 = ((bf16[64,10,512]{2,1,0:T(8,128)(2,1)}), bf16[64,10,512]{2,1,0:T(8,128)(2,1)S(1)}, u32[]{:S(2)}, u32[]{:S(2)}) async-start(bf16[64,10,512]{2,1,0:T(8,128)(2,1)} %reshape.255), calls=%async_computation.1 | async-start | bytes 2097152 | tf_op jit(solution)/shard_map/all_to_all | solution.py:358
Sparse Core Ops, SparseCore 0:
  10.1 83.4 all-gather.1
